TPU v7x, 32 devices: a whole 2x2x4 slice. The times are simulated.
32 devices in a mesh: dp: 16 (over z, y, core), tensor: 2 (over x).
Axes of the slice: x: 2, y: 2, z: 4, core: 2. Of those that a mesh axis runs over, the one named last changes fastest.
Arguments:
- hidden_in: float32 [16384, 768], P(('dp', 'tensor')), may hold values from -6 to 6
- cotangent: float32 [16384, 768], P(('dp', 'tensor')), may hold values from -6 to 6
- proj_zx: float32 [768, 2, 1536], P('dp', None, 'tensor'), may hold values from -0.21875 to 0.21875
- proj_dt: float32 [768, 24], P('dp', 'tensor'), may hold values from -0.21875 to 0.21875
- proj_bc: float32 [768, 256], P('dp'), may hold values from -0.21875 to 0.21875
- proj_out: float32 [768, 1536], P('dp', 'tensor'), may hold values from -0.15625 to 0.15625
- norm_gain: float32 [768], replicated, may hold values from 0.5 to 1.5
- conv_inner: float32 [5, 1536], P(None, 'tensor'), may hold values from -0.5 to 0.5
- conv_shared: float32 [5, 256], replicated, may hold values from -0.5 to 0.5
- head_table: float32 [3, 24], P(None, 'tensor'), may hold values from -7 to 3, as said below
- gate_gain: float32 [1536], P('tensor'), may hold values from 0.5 to 1.5
- mom_zx: float32 [768, 2, 1536], P('dp', None, 'tensor'), may hold values from -76.8 to 76.8
- mom_dt: float32 [768, 24], P('dp', 'tensor'), may hold values from -76.8 to 76.8
- mom_bc: float32 [768, 256], P('dp'), may hold values from -76.8 to 76.8
- mom_out: float32 [768, 1536], P('dp', 'tensor'), may hold values from -76.8 to 76.8
- mom_norm: float32 [768], replicated, may hold values from -76.8 to 76.8
- mom_conv: float32 [5, 1536], P(None, 'tensor'), may hold values from -76.8 to 76.8
- mom_shared: float32 [5, 256], replicated, may hold values from -76.8 to 76.8
- mom_head: float32 [3, 24], P(None, 'tensor'), may hold values from -76.8 to 76.8
- mom_gate: float32 [1536], P('tensor'), may hold values from -76.8 to 76.8
- var_zx: float32 [768, 2, 1536], P('dp', None, 'tensor'), may hold values from 16.384 to 1638.4
- var_dt: float32 [768, 24], P('dp', 'tensor'), may hold values from 16.384 to 1638.4
- var_bc: float32 [768, 256], P('dp'), may hold values from 16.384 to 1638.4
- var_out: float32 [768, 1536], P('dp', 'tensor'), may hold values from 16.384 to 1638.4
- var_norm: float32 [768], replicated, may hold values from 16.384 to 1638.4
- var_conv: float32 [5, 1536], P(None, 'tensor'), may hold values from 16.384 to 1638.4
- var_shared: float32 [5, 256], replicated, may hold values from 16.384 to 1638.4
- var_head: float32 [3, 24], P(None, 'tensor'), may hold values from 16.384 to 1638.4
- var_gate: float32 [1536], P('tensor'), may hold values from 16.384 to 1638.4
Outputs:
- hidden_out: float32 [16384, 768], P(('dp', 'tensor'))
- grad_hidden: float32 [16384, 768], P(('dp', 'tensor'))
- grad_zx: float32 [768, 2, 1536], P('dp', None, 'tensor')
- grad_dt: float32 [768, 24], P('dp', 'tensor')
- grad_bc: float32 [768, 256], P('dp')
- grad_out: float32 [768, 1536], P('dp', 'tensor')
- grad_norm: float32 [768], replicated
- grad_conv: float32 [5, 1536], P(None, 'tensor')
- grad_shared: float32 [5, 256], replicated
- grad_head: float32 [3, 24], P(None, 'tensor')
- grad_gate: float32 [1536], P('tensor')
- new_zx: float32 [768, 2, 1536], P('dp', None, 'tensor')
- new_dt: float32 [768, 24], P('dp', 'tensor')
- new_bc: float32 [768, 256], P('dp')
- new_out: float32 [768, 1536], P('dp', 'tensor')
- new_norm: float32 [768], replicated
- new_conv: float32 [5, 1536], P(None, 'tensor')
- new_shared: float32 [5, 256], replicated
- new_head: float32 [3, 24], P(None, 'tensor')
- new_gate: float32 [1536], P('tensor')
- new_mom_zx: float32 [768, 2, 1536], P('dp', None, 'tensor')
- new_mom_dt: float32 [768, 24], P('dp', 'tensor')
- new_mom_bc: float32 [768, 256], P('dp')
- new_mom_out: float32 [768, 1536], P('dp', 'tensor')
- new_mom_norm: float32 [768], replicated
- new_mom_conv: float32 [5, 1536], P(None, 'tensor')
- new_mom_shared: float32 [5, 256], replicated
- new_mom_head: float32 [3, 24], P(None, 'tensor')
- new_mom_gate: float32 [1536], P('tensor')
- new_var_zx: float32 [768, 2, 1536], P('dp', None, 'tensor')
- new_var_dt: float32 [768, 24], P('dp', 'tensor')
- new_var_bc: float32 [768, 256], P('dp')
- new_var_out: float32 [768, 1536], P('dp', 'tensor')
- new_var_norm: float32 [768], replicated
- new_var_conv: float32 [5, 1536], P(None, 'tensor')
- new_var_shared: float32 [5, 256], replicated
- new_var_head: float32 [3, 24], P(None, 'tensor')
- new_var_gate: float32 [1536], P('tensor')
Inputs may be any that keep to these rules, and one draw needn't show every extreme that they name: `head_table`: row 0 holds step size offsets, row 1 logarithms of decay rates, row 2 skip gains.
All inputs are finite; a program needn't handle non-finite values.
Results may differ from a plain program's by a relative error of at most 0.0033.
The roundings to bfloat16 on the way count: a program that leaves them out, or rounds other values in their place, can miss the bound.
Values may be sent and summed in bfloat16 or wider, within the bound.
A program may use at most 192 MiB of HBM per device.

v0:
```python
import jax
import jax.numpy as jnp
from jax import lax
from jax.sharding import PartitionSpec as P

HEADS = 24
HEAD_DIM = 64
SPAN = 256
LEN = 512
STEP = 3
INNER = 1536
epsilon = 1e-05
precise = lax.Precision.HIGHEST
beta_first = 0.9
beta_second = 0.95
learn_rate = 0.1
weight_decay = 0.01
adam_epsilon = 1e-08


def conv_silu(values, kernel, seq_count):
    kernel_taps = kernel.shape[0] - 1
    shaped = values.reshape(seq_count, LEN, values.shape[1])
    padded = jnp.pad(shaped, ((0, 0), (kernel_taps - 1, 0), (0, 0)))
    summed = kernel[kernel_taps] + jnp.zeros_like(shaped)
    for offset in range(kernel_taps):
        summed = summed + kernel[offset] * padded[:, offset : offset + LEN]
    return jax.nn.silu(summed).reshape(values.shape)


def state_space(values, step_size, decay_rate, key_rows, query_rows):
    seq_count = values.shape[0] // LEN
    blocks = LEN // SPAN
    head_count = step_size.shape[1]
    state_dim = key_rows.shape[1]
    block_x = values.reshape(seq_count, blocks, SPAN, head_count, HEAD_DIM)
    block_dt = step_size.reshape(seq_count, blocks, SPAN, head_count)
    block_b = key_rows.reshape(seq_count, blocks, SPAN, state_dim)
    block_c = query_rows.reshape(seq_count, blocks, SPAN, state_dim)
    cumul = jnp.cumsum(block_dt * decay_rate, axis=2)
    position = jnp.arange(SPAN)
    lower_mask = (position[:, None] >= position[None, :])[:, :, None]
    spread = cumul[:, :, :, None, :] - cumul[:, :, None, :, :]
    within = jnp.where(lower_mask, jnp.exp(jnp.where(lower_mask, spread, 0.0)), 0.0)
    scores = jnp.einsum("bcin,bcjn->bcij", block_c, block_b, precision=precise)
    weighted = block_x * block_dt[..., None]
    mixing_table = scores[..., None] * within
    diag_part = jnp.einsum("bcijh,bcjhp->bcihp", mixing_table, weighted, precision=precise)
    to_end = jnp.exp(cumul[:, :, -1:, :] - cumul)
    states = jnp.einsum(
        "bcjn,bcjhp->bchpn", block_b, to_end[..., None] * weighted, precision=precise
    )
    whole_decay = jnp.exp(cumul[:, :, -1, :])

    def advance(running, inputs):
        block_state, block_decay = inputs
        return (running * block_decay[:, :, None, None] + block_state, running)

    zero_state = jnp.zeros((seq_count, head_count, HEAD_DIM, state_dim), jnp.float32)
    final_state, entering = lax.scan(
        advance, zero_state, (jnp.moveaxis(states, 1, 0), jnp.moveaxis(whole_decay, 1, 0))
    )
    entering = jnp.moveaxis(entering, 0, 1)
    off_part = (
        jnp.einsum("bcin,bchpn->bcihp", block_c, entering, precision=precise)
        * jnp.exp(cumul)[..., None]
    )
    return (diag_part + off_part).reshape(seq_count * LEN, head_count * HEAD_DIM)


def mixing(x_raw, bc_raw, dt_raw, conv_inner, conv_shared, head_table):
    seq_count = x_raw.shape[0] // LEN
    x_conv = conv_silu(x_raw, conv_inner, seq_count)
    bc_conv = conv_silu(bc_raw, conv_shared, seq_count)
    state_dim = bc_raw.shape[1] // 2
    step_size = jax.nn.softplus(dt_raw + head_table[0])
    decay_rate = -jnp.exp(head_table[1])
    result = state_space(
        x_conv, step_size, decay_rate, bc_conv[:, :state_dim], bc_conv[:, state_dim:]
    )
    return result + jnp.repeat(head_table[2], HEAD_DIM) * x_conv


def adam_update(weight, moment, second, gradient):
    moment_new = beta_first * moment + (1.0 - beta_first) * gradient
    second_new = beta_second * second + (1.0 - beta_second) * gradient * gradient
    corr_first = 1.0 - beta_first**STEP
    corr_second = 1.0 - beta_second**STEP
    update = moment_new / corr_first / (jnp.sqrt(second_new / corr_second) + adam_epsilon)
    return (weight - learn_rate * (update + weight_decay * weight), moment_new, second_new)


def widen_cols(piece_part, full_cols, position):
    zero_base = jnp.zeros(piece_part.shape[:-1] + (full_cols,), jnp.float32)
    return lax.dynamic_update_slice_in_dim(
        zero_base, piece_part, position * piece_part.shape[-1], piece_part.ndim - 1
    )


def on_device(
    hidden_in,
    cotangent,
    proj_zx,
    proj_dt,
    proj_bc,
    proj_out,
    norm_gain,
    conv_inner,
    conv_shared,
    head_table,
    gate_gain,
    mom_zx,
    mom_dt,
    mom_bc,
    mom_out,
    mom_norm,
    mom_conv,
    mom_shared,
    mom_head,
    mom_gate,
    var_zx,
    var_dt,
    var_bc,
    var_out,
    var_norm,
    var_conv,
    var_shared,
    var_head,
    var_gate,
):
    tensor_pos = lax.axis_index("tensor")
    local_rows = hidden_in.shape[0]
    inner_local = proj_out.shape[1]
    heads_local = proj_dt.shape[1]
    shard_rows = proj_zx.shape[0]
    scale_in = lax.rsqrt(jnp.mean(hidden_in * hidden_in, axis=-1, keepdims=True) + epsilon)
    unit_in = hidden_in * scale_in
    normed_local = (unit_in * norm_gain).astype(jnp.bfloat16)
    normed = lax.all_gather(normed_local, "tensor", axis=0, tiled=True)
    full_zx, full_dt, full_bc, full_out = (
        lax.all_gather(proj_zx.astype(jnp.bfloat16), "dp", axis=0, tiled=True),
        lax.all_gather(proj_dt.astype(jnp.bfloat16), "dp", axis=0, tiled=True),
        lax.all_gather(proj_bc.astype(jnp.bfloat16), "dp", axis=0, tiled=True),
        lax.all_gather(proj_out.astype(jnp.bfloat16), "dp", axis=0, tiled=True),
    )
    flat_zx = full_zx.reshape(full_zx.shape[0], 2 * inner_local)
    zx_raw = jnp.dot(normed, flat_zx, preferred_element_type=jnp.float32)
    gate_pre = zx_raw[:, :inner_local]
    x_raw = zx_raw[:, inner_local:]
    bc_raw = jnp.dot(normed, full_bc, preferred_element_type=jnp.float32)
    dt_raw = jnp.dot(normed, full_dt, preferred_element_type=jnp.float32)
    mixer_out, pullback = jax.vjp(
        mixing, x_raw, bc_raw, dt_raw, conv_inner, conv_shared, head_table
    )
    gate_act = jax.nn.silu(gate_pre)
    gated_out = mixer_out * gate_act
    square_sum = lax.psum(jnp.sum(gated_out * gated_out, axis=-1), "tensor")
    scale_gate = lax.rsqrt(square_sum / INNER + epsilon)[:, None]
    unit_gate = gated_out * scale_gate
    normed_gate = (unit_gate * gate_gain).astype(jnp.bfloat16)
    cot_local = cotangent.astype(jnp.bfloat16)
    branch_out = lax.psum_scatter(
        jnp.dot(normed_gate, full_out.T, preferred_element_type=jnp.float32),
        "tensor",
        scatter_dimension=0,
        tiled=True,
    )
    cot_all = lax.all_gather(cot_local, "tensor", axis=0, tiled=True)
    d_gate_out = jnp.dot(cot_all, full_out, preferred_element_type=jnp.float32)
    grad_out_group = jnp.dot(cot_all.T, normed_gate, preferred_element_type=jnp.float32)
    hidden_out = hidden_in + branch_out
    gate_part = jnp.sum(d_gate_out * unit_gate, axis=0)
    d_unit = d_gate_out * gate_gain
    inner_dot = lax.psum(jnp.sum(d_unit * unit_gate, axis=-1), "tensor")
    d_gated = scale_gate * (d_unit - unit_gate * (inner_dot / INNER)[:, None])
    d_mixer = d_gated * gate_act
    sigm = jax.nn.sigmoid(gate_pre)
    d_gate_pre = d_gated * mixer_out * sigm * (1.0 + gate_pre * (1.0 - sigm))
    d_x_raw, d_bc_part, d_dt_raw, conv_part, shared_part, head_part = pullback(d_mixer)
    d_bc_raw = lax.psum(d_bc_part, "tensor")
    d_zx16 = jnp.concatenate([d_gate_pre, d_x_raw], axis=1).astype(jnp.bfloat16)
    d_dt16 = d_dt_raw.astype(jnp.bfloat16)
    d_bc16 = d_bc_raw.astype(jnp.bfloat16)
    partial_in = jnp.dot(d_zx16, flat_zx.T, preferred_element_type=jnp.float32)
    partial_in = partial_in + jnp.dot(d_dt16, full_dt.T, preferred_element_type=jnp.float32)
    d_normed = lax.psum_scatter(partial_in, "tensor", scatter_dimension=0, tiled=True)
    own_bc = lax.dynamic_slice_in_dim(d_bc16, tensor_pos * local_rows, local_rows, 0)
    d_normed = d_normed + jnp.dot(own_bc, full_bc.T, preferred_element_type=jnp.float32)
    zx_group = jnp.dot(normed.T, d_zx16, preferred_element_type=jnp.float32).reshape(
        flat_zx.shape[0], 2, inner_local
    )
    dt_group = jnp.dot(normed.T, d_dt16, preferred_element_type=jnp.float32)
    norm_part = jnp.sum(d_normed * unit_in, axis=0)
    d_unit_in = d_normed * norm_gain
    grad_hidden = cotangent + scale_in * (
        d_unit_in - unit_in * jnp.mean(d_unit_in * unit_in, axis=-1, keepdims=True)
    )
    wide_conv = widen_cols(conv_part, INNER, tensor_pos)
    wide_gate = widen_cols(gate_part, INNER, tensor_pos)
    wide_head = widen_cols(head_part, HEADS, tensor_pos)
    bc_own = jnp.dot(normed_local.T, own_bc, preferred_element_type=jnp.float32)
    grad_zx, grad_dt, grad_out = (
        lax.psum_scatter(zx_group, "dp", scatter_dimension=0, tiled=True),
        lax.psum_scatter(dt_group, "dp", scatter_dimension=0, tiled=True),
        lax.psum_scatter(grad_out_group, "dp", scatter_dimension=0, tiled=True),
    )
    sum_norm, sum_shared, sum_conv, sum_gate, sum_head, sum_bc = lax.psum(
        (norm_part, shared_part, wide_conv, wide_gate, wide_head, bc_own), ("dp", "tensor")
    )
    grad_bc = lax.dynamic_slice_in_dim(sum_bc, lax.axis_index("dp") * shard_rows, shard_rows, 0)
    grad_conv = lax.dynamic_slice_in_dim(sum_conv, tensor_pos * inner_local, inner_local, 1)
    grad_gate = lax.dynamic_slice_in_dim(sum_gate, tensor_pos * inner_local, inner_local, 0)
    grad_head = lax.dynamic_slice_in_dim(sum_head, tensor_pos * heads_local, heads_local, 1)
    grads = (
        grad_zx,
        grad_dt,
        grad_bc,
        grad_out,
        sum_norm,
        grad_conv,
        sum_shared,
        grad_head,
        grad_gate,
    )
    weights = (
        proj_zx,
        proj_dt,
        proj_bc,
        proj_out,
        norm_gain,
        conv_inner,
        conv_shared,
        head_table,
        gate_gain,
    )
    moments = (mom_zx, mom_dt, mom_bc, mom_out, mom_norm, mom_conv, mom_shared, mom_head, mom_gate)
    seconds = (var_zx, var_dt, var_bc, var_out, var_norm, var_conv, var_shared, var_head, var_gate)
    results = [
        adam_update(w_item, m_item, v_item, g_item)
        for w_item, m_item, v_item, g_item in zip(weights, moments, seconds, grads)
    ]
    new_weights = tuple((item[0] for item in results))
    new_moments = tuple((item[1] for item in results))
    new_seconds = tuple((item[2] for item in results))
    return (hidden_out, grad_hidden) + grads + new_weights + new_moments + new_seconds


def solution(mesh):
    placed = (
        P(("dp", "tensor"), None),
        P(("dp", "tensor"), None),
        P("dp", None, "tensor"),
        P("dp", "tensor"),
        P("dp", None),
        P("dp", "tensor"),
        P(),
        P(None, "tensor"),
        P(),
        P(None, "tensor"),
        P("tensor"),
        P("dp", None, "tensor"),
        P("dp", "tensor"),
        P("dp", None),
        P("dp", "tensor"),
        P(),
        P(None, "tensor"),
        P(),
        P(None, "tensor"),
        P("tensor"),
        P("dp", None, "tensor"),
        P("dp", "tensor"),
        P("dp", None),
        P("dp", "tensor"),
        P(),
        P(None, "tensor"),
        P(),
        P(None, "tensor"),
        P("tensor"),
    )
    return jax.shard_map(
        on_device,
        mesh=mesh,
        in_specs=placed,
        out_specs=(
            P(("dp", "tensor"), None),
            P(("dp", "tensor"), None),
            P("dp", None, "tensor"),
            P("dp", "tensor"),
            P("dp", None),
            P("dp", "tensor"),
            P(),
            P(None, "tensor"),
            P(),
            P(None, "tensor"),
            P("tensor"),
            P("dp", None, "tensor"),
            P("dp", "tensor"),
            P("dp", None),
            P("dp", "tensor"),
            P(),
            P(None, "tensor"),
            P(),
            P(None, "tensor"),
            P("tensor"),
            P("dp", None, "tensor"),
            P("dp", "tensor"),
            P("dp", None),
            P("dp", "tensor"),
            P(),
            P(None, "tensor"),
            P(),
            P(None, "tensor"),
            P("tensor"),
            P("dp", None, "tensor"),
            P("dp", "tensor"),
            P("dp", None),
            P("dp", "tensor"),
            P(),
            P(None, "tensor"),
            P(),
            P(None, "tensor"),
            P("tensor"),
        ),
        check_vma=False,
    )
```

profile of v0, /device:TPU:0, one launch (start us, length us, event | category | flops | bytes accessed | tf_op | source)
XLA Modules:
  0.0 886.6 jit_solution(6448583615369308812)
XLA Ops:
  14.2 23.3 %all-gather = bf16[16,48,12]{1,2,0:T(8,128)(2,1)S(1)} all-gather(bf16[1,48,12]{1,2,0:T(8,128)(2,1)S(1)} %convert_bitcast_fusion), channel_id=1, replica_groups=mesh['dp'=16,'tensor'=2] {'dp'}, dimensions={0}, use_global_device_ids=true | all-gather | bytes 19584 | tf_op jit(solution)/shard_map/all_gather | solution.py:142
  38.3 20.0 %all_gather.21 = bf16[768,256]{1,0:T(8,128)(2,1)} all-gather(bf16[48,256]{1,0:T(8,128)(2,1)S(1)} %convert_element_type.35), channel_id=1, replica_groups=mesh['dp'=16,'tensor'=2] {'dp'}, dimensions={0}, use_global_device_ids=true | all-gather | bytes 417792 | tf_op jit(solution)/shard_map/all_gather | solution.py:143
  73.0 13.7 %all-gather.8.cloned.1.call-done = bf16[768,2,768]{2,1,0:T(2,128)(2,1)} async-done(((bf16[48,2,768]{2,1,0:T(2,128)(2,1)}), bf16[768,2,768]{2,1,0:T(2,128)(2,1)}) %all-gather.8.cloned.1.call-update) | async-done | bytes 2359312 | tf_op jit(solution)/shard_map/all_gather | solution.py:141
  98.9 9.0 %fusion.29 = (f32[2,512,768]{1,2,0:T(8,128)}, f32[2,512,768]{1,2,0:T(8,128)}) fusion(f32[2,512,768]{1,2,0:T(8,128)} %copy.302, f32[768]{0:T(1024)S(1)} %copy-done.54, f32[768]{0:T(1024)S(1)} %get-tuple-element.591, f32[768]{0:T(1024)S(1)} %get-tuple-element.592, f32[768]{0:T(1024)S(1)} %get-tuple-element.593, f32[768]{0:T(1024)S(1)} %copy-done.72), kind=kLoop, calls=%fused_computation.66 | loop fusion | flops 9437184 | bytes 9452544 | tf_op jit(solution)/shard_map/jvp(jit(silu))/mul | solution.py:28
  132.6 14.3 %bitcast_add_fusion.3 = f32[2,2,256,12,64]{2,4,3,1,0:T(8,128)S(1)} fusion(f32[2,2,256,12,64]{2,4,3,1,0:T(8,128)S(1)} %fusion.64, f32[2,2,256,12]{2,3,1,0:T(8,128)S(1)} %bitcast.239, f32[2,2,256,256]{3,2,1,0:T(8,128)S(1)} %copy-done.26, pred[256,256]{1,0:T(8,128)(4,1)S(1)} %copy-done.47, f32[2,2,256,12,64]{2,1,4,3,0:T(2,128)S(1)} %copy-done.2, ...), kind=kOutput, calls=%fused_computation.48 | convolution fusion | flops 2430861312 | bytes 10698752 | tf_op jit(solution)/shard_map/jvp(bcijh,bcjhp->bcihp)/dot_general | solution.py:48
  160.0 6.4 multiply_reduce_fusion.9
  179.9 62.1 %reduce-scatter.15.cloned.1.call-done = f32[48,768]{1,0:T(8,128)} async-done(((f32[768,768]{1,0:T(8,128)}), f32[48,768]{1,0:T(8,128)}) %reduce-scatter.15.cloned.1.call-update) | async-done | bytes 147472
  243.9 38.2 %all-gather.10.cloned.1.call-done = bf16[768,768]{1,0:T(8,128)(2,1)} async-done(((bf16[48,768]{1,0:T(8,128)(2,1)}), bf16[768,768]{1,0:T(8,128)(2,1)}) %all-gather.10.cloned.1.call-update) | async-done | bytes 1179664 | tf_op jit(solution)/shard_map/all_gather | solution.py:144
  282.1 6.5 multiply_reduce_fusion
  294.9 8.9 %fusion.27 = (f32[768]{0:T(1024)}, f32[1024,768]{1,0:T(8,128)}, bf16[1024,768]{1,0:T(8,128)(2,1)}) fusion(f32[2,512,768]{2,1,0:T(8,128)} %copy.316, f32[1024,1536]{1,0:T(8,128)} %copy-done.5, f32[1024]{0:T(1024)S(1)} %broadcast_multiply_fusion.9, f32[1024,768]{1,0:T(8,128)} %get-tuple-element.665, f32[1024,768]{1,0:T(8,128)} %get-tuple-element.703, ...), kind=kLoop, calls=%fused_computation.47 | loop fusion | flops 16514304 | bytes 20464640 | tf_op jit(solution)/shard_map/transpose(jvp())/reduce_sum | solution.py:81
  329.7 9.1 %while.35 = (s32[]{:T(128)}, f32[2,12,64,128]{3,2,1,0:T(8,128)S(1)}, f32[2,2,12,64,128]{4,3,2,1,0:T(8,128)}, f32[2,2,12]{2,0,1:T(2,128)}, f32[2,2,12,64,128]{4,3...) while((s32[]{:T(128)}, ...), condition=%wide.region_12.13_spmd.clone, body=%wide.region_10.12_spmd.clone.sunk | while | flops 1179628 | bytes 4719300 | solution.py:60
  349.2 19.4 %fusion.12 = (f32[2,2,256,12]{2,3,1,0:T(8,128)}, f32[2,2,256,12]{2,3,1,0:T(8,128)}, f32[2,2,256,256]{3,2,1,0:T(8,128)S(1)}) fusion(f32[2,2,256,12]{2,3,1,0:T(8,128)S(1)} %bitcast.240, f32[2,2,256,256]{3,2,1,0:T(8,128)S(1)} %copy-done.27, pred[256,256]{1,0:T(8,128)(4,1)S(1)} %copy-done.48, f32[2,2,256,12,64]{2,1,4,3,0:T(2,128)S(1)} %copy-done.3, ...), kind=kOutput, calls=%fused_computation.21 | convolution fusion | flops 2451021824 | bytes 8650752 | tf_op jit(solution)/shard_map/transpose(jvp(bcijh,bcjhp->bcihp))/dot_general | solution.py:48
  368.6 13.6 %multiply_reduce_fusion.5 = (f32[2,2,256,12]{2,3,1,0:T(8,128)S(1)}, f32[2,2,256,12]{2,3,1,0:T(8,128)}, f32[2,2,256,12,64]{2,4,3,1,0:T(8,128)}) fusion(f32[2,2,256,12,64]{2,4,3,1,0:T(8,128)S(1)} %fusion.61, f32[2,2,256,12,64]{2,1,4,3,0:T(2,128)S(1)} %copy-done.3, f32[2,2,256,12]{2,3,1,0:T(8,128)S(1)} %copy-done.30, f32[2,2,256,12]{2,3,1,0:T(8,128)S(1)} %bitcast.241, ...), kind=kOutput, calls=%fused_computation.54 | convolution fusion | flops 2434768896 | bytes 13942784 | tf_op jit(solution)/shard_map/transpose(jvp(bcijh,bcjhp->bcihp))/dot_general | solution.py:48
  385.8 9.9 %reduce-window.16 = f32[2,2,12,2,128]{4,2,3,1,0:T(8,128)S(1)} reduce-window(f32[2,2,12,2,128]{4,2,3,1,0:T(8,128)S(1)} %copy.337, f32[]{:T(128)} %constant.87.clone.1), window={size=1x1x1x1x128 pad=0_0x0_0x0_0x0_0x0_127}, to_apply=%region_19.20 | reduce-window | flops 1560576 | bytes 98308 | tf_op jit(solution)/shard_map/reduce-window.2
  429.8 27.6 %all-reduce.36 = bf16[1024,256]{1,0:T(8,128)(2,1)S(1)} all-reduce(f32[1024,256]{1,0:T(8,128)S(1)} %bitcast.230), channel_id=1, replica_groups=mesh['dp'=16,'tensor'=2] {'tensor'}, use_global_device_ids=true, to_apply=%region_23.24 | all-reduce | flops 262144 | bytes 1572864 | tf_op jit(solution)/shard_map/psum | solution.py:180
  457.4 9.9 %multiply_reduce_fusion.4 = (f32[768]{0:T(1024)}, f32[768]{0:T(1024)S(1)}, f32[768]{0:T(1024)}, f32[768]{0:T(1024)}, f32[768]{0:T(1024)S(1)}, /*index=5*/f32[2,512,768]{1,2,0:T(8,128)S(1)}) fusion(f32[2,512,768]{1,2,0:T(8,128)} %copy.302, f32[2,512,768]{1,2,0:T(8,128)} %get-tuple-element.667, f32[2,512,768]{1,2,0:T(8,128)} %copy.325), kind=kLoop, calls=%fused_computation.53 | loop fusion | flops 14151936 | bytes 12598272 | tf_op jit(solution)/shard_map/transpose(jvp())/reduce_sum | solution.py:27
  475.3 8.4 fusion.25
  486.3 6.2 fusion.39
  492.5 6.6 reshape.313
  521.2 7.1 reduce-scatter.13.cloned.1.call-done
  531.1 131.4 %all-reduce.33.cloned.1.call-done = f32[768,256]{1,0:T(8,128)} async-done(((f32[768,256]{1,0:T(8,128)}), f32[768,256]{1,0:T(8,128)}) %all-reduce.33.cloned.1.call-update) | async-done | bytes 786448 | tf_op jit(solution)/shard_map/psum | solution.py:207
  664.0 118.0 %all-reduce.35.cloned.1.call-done = f32[768,2,768]{2,1,0:T(2,128)} async-done(((f32[768,2,768]{2,1,0:T(2,128)}), f32[768,2,768]{2,1,0:T(2,128)}) %all-reduce.35.cloned.1.call-update) | async-done | bytes 4718608
  785.1 42.4 %reduce-scatter.11.cloned.1.call-done = f32[512,768]{1,0:T(8,128)} async-done(((f32[1024,768]{1,0:T(8,128)}), f32[512,768]{1,0:T(8,128)}) %reduce-scatter.11.cloned.1.call-update) | async-done | bytes 1572880 | tf_op jit(solution)/shard_map/reduce_scatter | solution.py:186
  830.6 41.4 %all-reduce.28 = (f32[768]{0:T(1024)S(1)}, f32[5,1536]{1,0:T(8,128)S(1)}, f32[5,256]{1,0:T(8,128)S(1)}, f32[3,24]{1,0:T(4,128)S(1)}, f32[1536]{0:T(1024)S(1)}) all-reduce(f32[768]{0:T(1024)S(1)} %get-tuple-element.577, f32[5,1536]{1,0:T(8,128)S(1)} %add_dynamic-update-slice_fusion, ...), channel_id=1, replica_groups=mesh['dp'=16,'tensor'=2] {'dp','tensor'}, use_global_device_ids=true, to_apply=%region_30.31 | all-reduce | flops 11336 | bytes 90688 | tf_op jit(solution)/shard_map/psum | solution.py:207
  (384 shorter events, 229.1 us)
Async XLA Ops:
  7.2 51.8 %all-gather.6.cloned.1.call-start = ((), (), s32[]{:S(2)}) async-start(), calls=%async_computation.4 | async-start | bytes 2359296 | tf_op jit(solution)/shard_map/all_gather | solution.py:139
  11.6 75.1 %all-gather.8.cloned.1.call-start = ((), (), s32[]{:S(2)}) async-start(), calls=%async_computation.5 | async-start | bytes 2506752 | tf_op jit(solution)/shard_map/all_gather | solution.py:141
  12.4 159.0 %all-gather.12.cloned.1.call-start = ((), (), s32[]{:S(2)}) async-start(), calls=%async_computation.8 | async-start | bytes 2359296 | tf_op jit(solution)/shard_map/all_gather | solution.py:168
  13.5 228.5 %reduce-scatter.15.cloned.1.call-start = ((), (), s32[]{:S(2)}) async-start(), calls=%async_computation.12 | async-start | bytes 2506752
  171.4 123.5 %copy-start.56 = (f32[1024]{0:T(1024)}, f32[1024]{0:T(1024)S(1)}, u32[]{:S(2)}) copy-start(f32[1024]{0:T(1024)S(1)} %add_rsqrt_fusion) | copy-start | bytes 12292
  179.9 102.2 %all-gather.10.cloned.1.call-start = ((), (), s32[]{:S(2)}) async-start(), calls=%async_computation.6 | async-start | bytes 1253376 | tf_op jit(solution)/shard_map/all_gather | solution.py:144
  243.8 284.5 %reduce-scatter.13.cloned.1.call-start = ((), (), s32[]{:S(2)}) async-start(), calls=%async_computation.11 | async-start | bytes 417792
  473.9 188.6 %all-reduce.33.cloned.1.call-start = ((), (), s32[]{:S(2)}) async-start(), calls=%async_computation.10 | async-start | bytes 1572864 | tf_op jit(solution)/shard_map/psum | solution.py:207
  486.3 295.7 %all-reduce.35.cloned.1.call-start = ((), (), s32[]{:S(2)}) async-start(), calls=%async_computation.13 | async-start | bytes 9437184
  499.2 328.3 %reduce-scatter.11.cloned.1.call-start = ((), (), s32[]{:S(2)}) async-start(), calls=%async_computation.9 | async-start | bytes 4718592 | tf_op jit(solution)/shard_map/reduce_scatter | solution.py:186
  507.7 367.2 %reduce-scatter.9.cloned.1.call-start = ((), (), s32[]{:S(2)}) async-start(), calls=%async_computation.7 | async-start | bytes 4718592 | tf_op jit(solution)/shard_map/reduce_scatter | solution.py:162
  514.1 148.4 %copy-start.42 = (f32[48,256]{1,0:T(8,128)S(1)}, f32[48,256]{1,0:T(8,128)}, u32[]{:S(2)}) copy-start(f32[48,256]{1,0:T(8,128)} %param.37) | copy-start | bytes 147460
  514.1 148.4 %copy-start.51 = (f32[48,256]{1,0:T(8,128)S(1)}, f32[48,256]{1,0:T(8,128)}, u32[]{:S(2)}) copy-start(f32[48,256]{1,0:T(8,128)} %param.46) | copy-start | bytes 147460
  514.1 267.9 %copy-start.24 = (f32[48,2,768]{2,1,0:T(2,128)S(1)}, f32[48,2,768]{2,1,0:T(2,128)}, u32[]{:S(2)}) copy-start(f32[48,2,768]{2,1,0:T(2,128)} %param.35) | copy-start | bytes 884740
  514.1 267.9 %copy-start.35 = (f32[48,2,768]{2,1,0:T(2,128)S(1)}, f32[48,2,768]{2,1,0:T(2,128)}, u32[]{:S(2)}) copy-start(f32[48,2,768]{2,1,0:T(2,128)} %param.44) | copy-start | bytes 884740
  514.1 267.9 %copy-start.36 = (f32[48,2,768]{2,1,0:T(2,128)S(1)}, f32[48,2,768]{2,1,0:T(2,128)}, u32[]{:S(2)}) copy-start(f32[48,2,768]{2,1,0:T(2,128)} %param.53) | copy-start | bytes 884740
  514.1 313.4 %copy-start.4 = (f32[512,768]{1,0:T(8,128)S(1)}, f32[512,768]{1,0:T(8,128)}, u32[]{:S(2)}) copy-start(f32[512,768]{1,0:T(8,128)} %param.33) | copy-start | bytes 4718596
  514.1 313.4 %copy-start.19 = (bf16[768,256]{1,0:T(8,128)(2,1)S(1)}, bf16[768,256]{1,0:T(8,128)(2,1)}, u32[]{:S(2)}) copy-start(bf16[768,256]{1,0:T(8,128)(2,1)} %all_gather.21) | copy-start | bytes 1179652
  514.1 313.4 %copy-start.46 = (f32[768]{0:T(1024)S(1)}, f32[768]{0:T(1024)}, u32[]{:S(2)}) copy-start(f32[768]{0:T(1024)} %param.39) | copy-start | bytes 9220
  785.0 88.5 %copy-start.99 = (f32[768]{0:T(1024)S(1)}, f32[768]{0:T(1024)}, u32[]{:S(2)}) copy-start(f32[768]{0:T(1024)} %param.52) | copy-start | bytes 9220
  785.1 89.1 %copy-start.50 = (f32[5,768]{1,0:T(8,128)S(1)}, f32[5,768]{1,0:T(8,128)}, u32[]{:S(2)}) copy-start(f32[5,768]{1,0:T(8,128)} %param.40) | copy-start | bytes 46084
  785.1 89.1 %copy-start.67 = (f32[5,768]{1,0:T(8,128)S(1)}, f32[5,768]{1,0:T(8,128)}, u32[]{:S(2)}) copy-start(f32[5,768]{1,0:T(8,128)} %param.49) | copy-start | bytes 46084
  785.1 89.1 %copy-start.68 = (f32[5,768]{1,0:T(8,128)S(1)}, f32[5,768]{1,0:T(8,128)}, u32[]{:S(2)}) copy-start(f32[5,768]{1,0:T(8,128)} %param.58) | copy-start | bytes 46084
  785.1 89.8 %copy-start.65 = (f32[512]{0:T(512)S(1)}, f32[512]{0:T(512)}, u32[]{:S(2)}) copy-start(f32[512]{0:T(512)} %copy-done.64) | copy-start | bytes 6148
  (94 other events, 1692.3 us)
Sparse Core Ops, SparseCore 0:
  11.7 29.8 all-gather.5
  44.5 42.1 all-gather.7
  88.8 25.8 all-gather.11
  180.0 61.9 reduce-scatter.14
  244.7 37.3 all-gather.9
  474.0 54.2 reduce-scatter.12
  533.5 128.9 all-reduce.32
  666.1 115.8 all-reduce.34
  784.3 43.1 reduce-scatter.10
  829.6 44.7 reduce-scatter.8
where the time goes:
time: 898 us; the launch traced here: 887 us
  waiting for transfers between devices  413 us (46%)
  matrix products  129 us (14%)
  blocking collectives  123 us (14%)
  other arithmetic  110 us (12%)
  local copies, waits for them, and re-layouts  93.6 us (10%)
  between operations  16.5 us (2%)
    unnamed x13, waiting for transfers between devices  187 us
    psum x1, waiting for transfers between devices, on_device(): lax.psum((norm_part, shared_part, wide_conv, wide_gate, wide_head, bc_own...  131 us
    dot_general x3, matrix products, state_space(): jnp.einsum('bcijh,bcjhp->bcihp', mixing_table, weighted, precision=precise)  47.4 us
    reduce_scatter x1, waiting for transfers between devices, on_device(): lax.psum_scatter(partial_in, 'tensor', scatter_dimension=0, tiled=True)  42.4 us
    psum x1, blocking collectives, on_device(): lax.psum((norm_part, shared_part, wide_conv, wide_gate, wide_head, bc_own...  41.4 us
    all_gather x1, waiting for transfers between devices, on_device(): lax.all_gather(proj_out.astype(jnp.bfloat16), 'dp', axis=0, tiled=True)  38.2 us
    psum x1, blocking collectives, on_device(): d_bc_raw = lax.psum(d_bc_part, 'tensor')  27.6 us
    all_gather x1, blocking collectives, on_device(): lax.all_gather(proj_dt.astype(jnp.bfloat16), 'dp', axis=0, tiled=True)  23.3 us
  transfers between devices with their start and end apart: 10, of which 7 were waited for; matrix products, arithmetic and copies ran while one was open for 17% of the time, Pallas kernels for 0%

commit v1 on v0

--- a/solution.py
+++ b/solution.py
@@ -205,7 +205,7 @@
         lax.psum_scatter(grad_out_group, "dp", scatter_dimension=0, tiled=True),
     )
     sum_norm, sum_shared, sum_conv, sum_gate, sum_head, sum_bc = lax.psum(
-        (norm_part, shared_part, wide_conv, wide_gate, wide_head, bc_own), ("dp", "tensor")
+        lax.psum((norm_part, shared_part, wide_conv, wide_gate, wide_head, bc_own), "tensor"), "dp"
     )
     grad_bc = lax.dynamic_slice_in_dim(sum_bc, lax.axis_index("dp") * shard_rows, shard_rows, 0)
     grad_conv = lax.dynamic_slice_in_dim(sum_conv, tensor_pos * inner_local, inner_local, 1)

time: 898 us -> 832 us (0.927)
  waiting for transfers between devices: 413 us -> 339 us
  blocking collectives: 123 us -> 150 us
  local copies, waits for them, and re-layouts: 93.6 us -> 84.4 us
    psum x1, waiting for transfers between devices: 131 us -> 8.04 us  [on_device(): lax.psum((norm_part, shared_part, wide_conv, wide_gate, wide_head, bc_own...]
    psum x0 -> x1, blocking collectives: none -> 59.4 us  [on_device(): lax.psum(lax.psum((norm_part, shared_part, wide_conv, wide_gate, wide_hea...]
    unnamed x13, waiting for transfers between devices: 187 us -> 235 us
    psum x1, blocking collectives: 41.4 us -> 9.27 us  [on_device(): lax.psum((norm_part, shared_part, wide_conv, wide_gate, wide_head, bc_own...]
  transfers between devices with their start and end apart: 10 -> 10, of which waited for: 7 -> 7; matrix products, arithmetic and copies ran while one was open for 17% -> 18% of each run, Pallas kernels for 0% -> 0%
where the time goes in v1:
time: 832 us; the launch traced here: 821 us
  waiting for transfers between devices  339 us (41%)
  blocking collectives  150 us (18%)
  matrix products  123 us (15%)
  other arithmetic  106 us (13%)
  local copies, waits for them, and re-layouts  84.4 us (10%)
  between operations  16.6 us (2%)
    unnamed x13, waiting for transfers between devices  235 us
    psum x1, blocking collectives, on_device(): lax.psum(lax.psum((norm_part, shared_part, wide_conv, wide_gate, wide_hea...  59.4 us
    dot_general x3, matrix products, state_space(): jnp.einsum('bcijh,bcjhp->bcihp', mixing_table, weighted, precision=precise)  47.4 us
    reduce_scatter x1, waiting for transfers between devices, on_device(): lax.psum_scatter(partial_in, 'tensor', scatter_dimension=0, tiled=True)  41.3 us
    all_gather x1, waiting for transfers between devices, on_device(): lax.all_gather(proj_out.astype(jnp.bfloat16), 'dp', axis=0, tiled=True)  38.2 us
    psum x1, blocking collectives, on_device(): d_bc_raw = lax.psum(d_bc_part, 'tensor')  28.7 us
    all_gather x1, blocking collectives, on_device(): lax.all_gather(proj_dt.astype(jnp.bfloat16), 'dp', axis=0, tiled=True)  23.3 us
    another operation x8, other arithmetic  21.1 us
  transfers between devices with their start and end apart: 10, of which 7 were waited for; matrix products, arithmetic and copies ran while one was open for 18% of the time, Pallas kernels for 0%

profile of v1, /device:TPU:0, one launch (start us, length us, event | category | flops | bytes accessed | tf_op | source)
XLA Modules:
  0.0 820.8 jit_solution(2677232873614814329)
XLA Ops:
  14.3 23.3 %all-gather = bf16[16,48,12]{1,2,0:T(8,128)(2,1)S(1)} all-gather(bf16[1,48,12]{1,2,0:T(8,128)(2,1)S(1)} %convert_bitcast_fusion), channel_id=1, replica_groups=mesh['dp'=16,'tensor'=2] {'dp'}, dimensions={0}, use_global_device_ids=true | all-gather | bytes 19584 | tf_op jit(solution)/shard_map/all_gather | solution.py:142
  38.4 18.6 %all_gather.21 = bf16[768,256]{1,0:T(8,128)(2,1)S(1)} all-gather(bf16[48,256]{1,0:T(8,128)(2,1)S(1)} %convert_element_type.35), channel_id=1, replica_groups=mesh['dp'=16,'tensor'=2] {'dp'}, dimensions={0}, use_global_device_ids=true | all-gather | bytes 417792 | tf_op jit(solution)/shard_map/all_gather | solution.py:143
  70.0 16.9 %all-gather.8.cloned.1.call-done = bf16[768,2,768]{2,1,0:T(2,128)(2,1)} async-done(((bf16[48,2,768]{2,1,0:T(2,128)(2,1)}), bf16[768,2,768]{2,1,0:T(2,128)(2,1)}) %all-gather.8.cloned.1.call-update) | async-done | bytes 2359312 | tf_op jit(solution)/shard_map/all_gather | solution.py:141
  99.0 9.4 %fusion.29 = (f32[2,512,768]{1,2,0:T(8,128)}, f32[2,512,768]{1,2,0:T(8,128)}) fusion(f32[2,512,768]{1,2,0:T(8,128)} %copy.302, f32[768]{0:T(1024)S(1)} %copy-done.61, f32[768]{0:T(1024)S(1)} %get-tuple-element.591, f32[768]{0:T(1024)S(1)} %get-tuple-element.592, f32[768]{0:T(1024)S(1)} %get-tuple-element.593, f32[768]{0:T(1024)S(1)} %copy-done.76), kind=kLoop, calls=%fused_computation.66 | loop fusion | flops 9437184 | bytes 9452544 | tf_op jit(solution)/shard_map/jvp(jit(silu))/mul | solution.py:28
  132.0 14.3 %bitcast_add_fusion.3 = f32[2,2,256,12,64]{2,4,3,1,0:T(8,128)S(1)} fusion(f32[2,2,256,12,64]{2,4,3,1,0:T(8,128)S(1)} %fusion.64, f32[2,2,256,12]{2,3,1,0:T(8,128)S(1)} %bitcast.239, f32[2,2,256,256]{3,2,1,0:T(8,128)S(1)} %copy-done.31, pred[256,256]{1,0:T(8,128)(4,1)S(1)} %copy-done.53, f32[2,2,256,12,64]{2,1,4,3,0:T(2,128)S(1)} %copy-done.5, ...), kind=kOutput, calls=%fused_computation.48 | convolution fusion | flops 2430861312 | bytes 10698752 | tf_op jit(solution)/shard_map/jvp(bcijh,bcjhp->bcihp)/dot_general | solution.py:48
  159.7 6.5 multiply_reduce_fusion.9
  179.6 62.3 %reduce-scatter.15.cloned.1.call-done = f32[48,768]{1,0:T(8,128)} async-done(((f32[768,768]{1,0:T(8,128)}), f32[48,768]{1,0:T(8,128)}) %reduce-scatter.15.cloned.1.call-update) | async-done | bytes 147472
  243.8 38.2 %all-gather.10.cloned.1.call-done = bf16[768,768]{1,0:T(8,128)(2,1)} async-done(((bf16[48,768]{1,0:T(8,128)(2,1)}), bf16[768,768]{1,0:T(8,128)(2,1)}) %all-gather.10.cloned.1.call-update) | async-done | bytes 1179664 | tf_op jit(solution)/shard_map/all_gather | solution.py:144
  282.0 6.5 multiply_reduce_fusion
  294.8 8.9 %fusion.27 = (f32[768]{0:T(1024)}, f32[1024,768]{1,0:T(8,128)}, bf16[1024,768]{1,0:T(8,128)(2,1)}) fusion(f32[2,512,768]{2,1,0:T(8,128)} %copy.316, f32[1024,1536]{1,0:T(8,128)} %copy-done.10, f32[1024]{0:T(1024)S(1)} %broadcast_multiply_fusion.9, f32[1024,768]{1,0:T(8,128)} %get-tuple-element.672, f32[1024,768]{1,0:T(8,128)} %get-tuple-element.710, ...), kind=kLoop, calls=%fused_computation.47 | loop fusion | flops 16514304 | bytes 20464640 | tf_op jit(solution)/shard_map/transpose(jvp())/reduce_sum | solution.py:81
  329.6 9.0 %while.35 = (s32[]{:T(128)}, f32[2,12,64,128]{3,2,1,0:T(8,128)S(1)}, f32[2,2,12,64,128]{4,3,2,1,0:T(8,128)}, f32[2,2,12]{2,0,1:T(2,128)}, f32[2,2,12,64,128]{4,3...) while((s32[]{:T(128)}, ...), condition=%wide.region_12.13_spmd.clone, body=%wide.region_10.12_spmd.clone.sunk | while | flops 1179628 | bytes 4719300 | solution.py:60
  348.3 19.4 %fusion.12 = (f32[2,2,256,12]{2,3,1,0:T(8,128)}, f32[2,2,256,12]{2,3,1,0:T(8,128)}, f32[2,2,256,256]{3,2,1,0:T(8,128)S(1)}) fusion(f32[2,2,256,12]{2,3,1,0:T(8,128)S(1)} %bitcast.240, f32[2,2,256,256]{3,2,1,0:T(8,128)S(1)} %copy-done.32, pred[256,256]{1,0:T(8,128)(4,1)S(1)} %copy-done.54, f32[2,2,256,12,64]{2,1,4,3,0:T(2,128)S(1)} %copy-done.6, ...), kind=kOutput, calls=%fused_computation.21 | convolution fusion | flops 2451021824 | bytes 8650752 | tf_op jit(solution)/shard_map/transpose(jvp(bcijh,bcjhp->bcihp))/dot_general | solution.py:48
  367.7 13.6 %multiply_reduce_fusion.5 = (f32[2,2,256,12]{2,3,1,0:T(8,128)S(1)}, f32[2,2,256,12]{2,3,1,0:T(8,128)}, f32[2,2,256,12,64]{2,4,3,1,0:T(8,128)}) fusion(f32[2,2,256,12,64]{2,4,3,1,0:T(8,128)S(1)} %fusion.61, f32[2,2,256,12,64]{2,1,4,3,0:T(2,128)S(1)} %copy-done.6, f32[2,2,256,12]{2,3,1,0:T(8,128)S(1)} %copy-done.35, f32[2,2,256,12]{2,3,1,0:T(8,128)S(1)} %bitcast.241, ...), kind=kOutput, calls=%fused_computation.54 | convolution fusion | flops 2434768896 | bytes 13942784 | tf_op jit(solution)/shard_map/transpose(jvp(bcijh,bcjhp->bcihp))/dot_general | solution.py:48
  383.6 9.9 %reduce-window.16 = f32[2,2,12,2,128]{4,2,3,1,0:T(8,128)S(1)} reduce-window(f32[2,2,12,2,128]{4,2,3,1,0:T(8,128)S(1)} %copy.337, f32[]{:T(128)} %constant.87.clone.1), window={size=1x1x1x1x128 pad=0_0x0_0x0_0x0_0x0_127}, to_apply=%region_19.20 | reduce-window | flops 1560576 | bytes 98308 | tf_op jit(solution)/shard_map/reduce-window.2
  419.5 28.7 %all-reduce.38 = bf16[1024,256]{1,0:T(8,128)(2,1)} all-reduce(f32[1024,256]{1,0:T(8,128)} %bitcast.230), channel_id=1, replica_groups=mesh['dp'=16,'tensor'=2] {'tensor'}, use_global_device_ids=true, to_apply=%region_23.24 | all-reduce | flops 262144 | bytes 1572864 | tf_op jit(solution)/shard_map/psum | solution.py:180
  448.1 6.2 multiply_reduce_fusion.4
  460.2 7.6 fusion.25
  477.9 6.8 reshape.313
  484.7 8.0 all-reduce.35.cloned.1.call-done
  510.0 42.8 %reduce-scatter.13.cloned.1.call-done = f32[48,12]{1,0:T(8,128)} async-done(((f32[768,12]{1,0:T(8,128)}), f32[48,12]{1,0:T(8,128)}) %reduce-scatter.13.cloned.1.call-update) | async-done | bytes 2320
  554.3 129.4 %all-reduce.37.cloned.1.call-done = (f32[768,2,768]{2,1,0:T(2,128)}, f32[768,256]{1,0:T(8,128)}) async-done(((f32[768,2,768]{2,1,0:T(2,128)}, f32[768,256]{1,0:T(8,128)}), (f32[768,2,768]{2,1,0:T(2,128)}, f32[768,256]{1,0:T(8,128)})) %all-reduce.37.cloned.1.call-update) | async-done | bytes 5505040
  688.2 41.3 %reduce-scatter.11.cloned.1.call-done = f32[512,768]{1,0:T(8,128)} async-done(((f32[1024,768]{1,0:T(8,128)}), f32[512,768]{1,0:T(8,128)}) %reduce-scatter.11.cloned.1.call-update) | async-done | bytes 1572880 | tf_op jit(solution)/shard_map/reduce_scatter | solution.py:186
  733.3 9.3 %all-reduce.30 = (f32[768]{0:T(1024)S(1)}, f32[5,1536]{1,0:T(8,128)S(1)}, f32[5,256]{1,0:T(8,128)S(1)}, f32[3,24]{1,0:T(4,128)S(1)}, f32[1536]{0:T(1024)S(1)}) all-reduce(f32[768]{0:T(1024)} %get-tuple-element.577, f32[5,1536]{1,0:T(8,128)} %copy-done.48, ...), channel_id=1, replica_groups=mesh['dp'=16,'tensor'=2] {'tensor'}, use_global_device_ids=true, to_apply=%region_31.32 | all-reduce | flops 11336 | bytes 90688 | tf_op jit(solution)/shard_map/psum | solution.py:208
  742.5 59.4 %all-reduce.28 = (f32[768]{0:T(1024)S(1)}, f32[5,1536]{1,0:T(8,128)S(1)}, f32[5,256]{1,0:T(8,128)S(1)}, f32[3,24]{1,0:T(4,128)S(1)}, f32[1536]{0:T(1024)S(1)}) all-reduce(f32[768]{0:T(1024)S(1)} %get-tuple-element.628, f32[5,1536]{1,0:T(8,128)S(1)} %get-tuple-element.629, ...), channel_id=1, replica_groups=mesh['dp'=16,'tensor'=2] {'dp'}, use_global_device_ids=true, to_apply=%region_32.33 | all-reduce | flops 11336 | bytes 90688 | tf_op jit(solution)/shard_map/psum | solution.py:207
  (380 shorter events, 220.2 us)
Async XLA Ops:
  7.2 49.9 %all-gather.6.cloned.1.call-start = ((), (), s32[]{:S(2)}) async-start(), calls=%async_computation.4 | async-start | bytes 2359296 | tf_op jit(solution)/shard_map/all_gather | solution.py:139
  11.6 75.3 %all-gather.8.cloned.1.call-start = ((), (), s32[]{:S(2)}) async-start(), calls=%async_computation.5 | async-start | bytes 2506752 | tf_op jit(solution)/shard_map/all_gather | solution.py:141
  12.4 158.6 %all-gather.12.cloned.1.call-start = ((), (), s32[]{:S(2)}) async-start(), calls=%async_computation.8 | async-start | bytes 2359296 | tf_op jit(solution)/shard_map/all_gather | solution.py:168
  13.5 228.4 %reduce-scatter.15.cloned.1.call-start = ((), (), s32[]{:S(2)}) async-start(), calls=%async_computation.12 | async-start | bytes 2506752
  171.0 123.8 %copy-start.63 = (f32[1024]{0:T(1024)}, f32[1024]{0:T(1024)S(1)}, u32[]{:S(2)}) copy-start(f32[1024]{0:T(1024)S(1)} %add_rsqrt_fusion) | copy-start | bytes 12292
  176.4 65.5 %copy-start.51 = (f32[48,768]{1,0:T(8,128)S(1)}, f32[48,768]{1,0:T(8,128)}, u32[]{:S(2)}) copy-start(f32[48,768]{1,0:T(8,128)} %param.56) | copy-start | bytes 442372
  179.6 102.4 %all-gather.10.cloned.1.call-start = ((), (), s32[]{:S(2)}) async-start(), calls=%async_computation.6 | async-start | bytes 1253376 | tf_op jit(solution)/shard_map/all_gather | solution.py:144
  243.7 249.0 %all-reduce.35.cloned.1.call-start = ((), (), s32[]{:S(2)}) async-start(), calls=%async_computation.10 | async-start | bytes 1572864 | tf_op jit(solution)/shard_map/psum | solution.py:208
  459.9 92.9 %reduce-scatter.13.cloned.1.call-start = ((), (), s32[]{:S(2)}) async-start(), calls=%async_computation.11 | async-start | bytes 417792
  472.1 211.6 %all-reduce.37.cloned.1.call-start = ((), (), s32[]{:S(2)}) async-start(), calls=%async_computation.13 | async-start | bytes 11010048
  492.7 236.7 %reduce-scatter.11.cloned.1.call-start = ((), (), s32[]{:S(2)}) async-start(), calls=%async_computation.9 | async-start | bytes 4718592 | tf_op jit(solution)/shard_map/reduce_scatter | solution.py:186
  499.4 310.1 %reduce-scatter.9.cloned.1.call-start = ((), (), s32[]{:S(2)}) async-start(), calls=%async_computation.7 | async-start | bytes 4718592 | tf_op jit(solution)/shard_map/reduce_scatter | solution.py:162
  505.8 177.9 %copy-start.47 = (f32[48,256]{1,0:T(8,128)S(1)}, f32[48,256]{1,0:T(8,128)}, u32[]{:S(2)}) copy-start(f32[48,256]{1,0:T(8,128)} %param.37) | copy-start | bytes 147460
  505.8 177.9 %copy-start.57 = (f32[48,256]{1,0:T(8,128)S(1)}, f32[48,256]{1,0:T(8,128)}, u32[]{:S(2)}) copy-start(f32[48,256]{1,0:T(8,128)} %param.46) | copy-start | bytes 147460
  505.8 177.9 %copy-start.58 = (f32[48,256]{1,0:T(8,128)S(1)}, f32[48,256]{1,0:T(8,128)}, u32[]{:S(2)}) copy-start(f32[48,256]{1,0:T(8,128)} %param.55) | copy-start | bytes 147460
  505.8 179.4 %copy-start.30 = (f32[48,2,768]{2,1,0:T(2,128)S(1)}, f32[48,2,768]{2,1,0:T(2,128)}, u32[]{:S(2)}) copy-start(f32[48,2,768]{2,1,0:T(2,128)} %param.35) | copy-start | bytes 884740
  505.9 179.3 %copy-start.40 = (f32[48,2,768]{2,1,0:T(2,128)S(1)}, f32[48,2,768]{2,1,0:T(2,128)}, u32[]{:S(2)}) copy-start(f32[48,2,768]{2,1,0:T(2,128)} %param.44) | copy-start | bytes 884740
  505.9 179.3 %copy-start.41 = (f32[48,2,768]{2,1,0:T(2,128)S(1)}, f32[48,2,768]{2,1,0:T(2,128)}, u32[]{:S(2)}) copy-start(f32[48,2,768]{2,1,0:T(2,128)} %param.53) | copy-start | bytes 884740
  505.9 223.5 %copy-start.7 = (f32[512,768]{1,0:T(8,128)S(1)}, f32[512,768]{1,0:T(8,128)}, u32[]{:S(2)}) copy-start(f32[512,768]{1,0:T(8,128)} %param.33) | copy-start | bytes 4718596
  505.9 223.5 %copy-start.20 = (bf16[768,256]{1,0:T(8,128)(2,1)S(1)}, bf16[768,256]{1,0:T(8,128)(2,1)}, u32[]{:S(2)}) copy-start(bf16[768,256]{1,0:T(8,128)(2,1)} %copy-done.19) | copy-start | bytes 1179652
  505.9 223.5 %copy-start.52 = (f32[768]{0:T(1024)S(1)}, f32[768]{0:T(1024)}, u32[]{:S(2)}) copy-start(f32[768]{0:T(1024)} %param.39) | copy-start | bytes 9220
  509.9 175.2 %copy-start.48 = (f32[5,1536]{1,0:T(8,128)}, f32[5,1536]{1,0:T(8,128)S(1)}, u32[]{:S(2)}) copy-start(f32[5,1536]{1,0:T(8,128)S(1)} %add_dynamic-update-slice_fusion) | copy-start | bytes 92164
  553.6 131.6 %copy-start.71 = (f32[48,12]{0,1:T(8,128)}, f32[48,12]{0,1:T(8,128)S(1)}, u32[]{:S(2)}) copy-start(f32[48,12]{0,1:T(8,128)S(1)} %copy.366) | copy-start | bytes 6916
  688.2 121.3 %copy-start.17 = (f32[512,768]{1,0:T(8,128)S(1)}, f32[512,768]{1,0:T(8,128)}, u32[]{:S(2)}) copy-start(f32[512,768]{1,0:T(8,128)} %param.34) | copy-start | bytes 4718596
  (91 other events, 943.4 us)
Sparse Core Ops, SparseCore 0:
  11.7 29.8 all-gather.5
  44.5 42.3 all-gather.7
  89.0 25.8 all-gather.11
  179.7 62.1 reduce-scatter.14
  244.6 37.3 all-gather.9
  460.0 32.6 all-reduce.34
  496.8 55.9 reduce-scatter.12
  556.5 127.1 all-reduce.36
  686.0 43.4 reduce-scatter.10
  731.5 44.0 reduce-scatter.8
